TPU v7x, 256 devices: a whole 4x4x8 slice. The times are simulated.
256 devices in a mesh: section: 4 (over z_lo), rep: 8 (over y, core), tp: 8 (over z_hi, x).
Axes of the slice: x: 4, y: 4, z: 8 (z_hi: 2, z_lo: 4; z = z_hi * 4 + z_lo), core: 2. Of those that a mesh axis runs over, the one named last changes fastest.
Arguments:
- acts: bfloat16 [8, 256, 896], P('rep', None, 'tp'), may hold values from -6 to 6
- cotangent: bfloat16 [8, 256, 896], P('rep', None, 'tp'), may hold values from -8.5 to 8.5
- w_gate: bfloat16 [4, 8, 896, 4864], P('section', 'rep', None, 'tp'), may hold values from -3 to 3
- w_up: bfloat16 [4, 8, 896, 4864], P('section', 'rep', None, 'tp'), may hold values from -3 to 3
- w_down: bfloat16 [4, 8, 4864, 896], P('section', 'rep', 'tp'), may hold values from -4.2 to 4.2
- m_gate: bfloat16 [4, 8, 896, 4864], P('section', 'rep', None, 'tp'), may hold values from -0.099609375 to 0.099609375
- m_up: bfloat16 [4, 8, 896, 4864], P('section', 'rep', None, 'tp'), may hold values from -0.099609375 to 0.099609375
- m_down: bfloat16 [4, 8, 4864, 896], P('section', 'rep', 'tp'), may hold values from -0.099609375 to 0.099609375
- v_gate: bfloat16 [4, 8, 896, 4864], P('section', 'rep', None, 'tp'), may hold values from 0.0009994507 to 0.099609375
- v_up: bfloat16 [4, 8, 896, 4864], P('section', 'rep', None, 'tp'), may hold values from 0.0009994507 to 0.099609375
- v_down: bfloat16 [4, 8, 4864, 896], P('section', 'rep', 'tp'), may hold values from 0.0009994507 to 0.099609375
- steps: int32 [4], P('section'), may hold values from 0 to 999
Outputs:
- section_out: bfloat16 [4, 8, 256, 896], P('section', 'rep', None, 'tp')
- section_in_grad: bfloat16 [4, 8, 256, 896], P('section', 'rep', None, 'tp')
- new_gate: bfloat16 [4, 8, 896, 4864], P('section', 'rep', None, 'tp')
- new_up: bfloat16 [4, 8, 896, 4864], P('section', 'rep', None, 'tp')
- new_down: bfloat16 [4, 8, 4864, 896], P('section', 'rep', 'tp')
All inputs are finite; a program needn't handle non-finite values.
Results may differ from a plain program's by a relative error of at most 0.023.
Values may be sent and summed in bfloat16 or wider, within the bound.
A program may use at most 128 MiB of HBM per device.

v0:
```python
import functools
import math
import jax
import jax.numpy as jnp
from jax import lax
from jax.sharding import PartitionSpec as P

D = 896
FF = 4864
TOK = 128
MB = 2
NORM_EPS = 1e-06
ADAM_EPS = 1e-08
LEARN = 0.3
BETA_ONE = 0.9
BETA_TWO = 0.95


def as_sent(array):
    return jax.tree.map(lambda a: a.astype(jnp.bfloat16) if a.dtype == jnp.float32 else a, array)


def from_behind(array, axis, by):
    peers = lax.axis_size(axis)
    return lax.ppermute(array, axis, [(i, (i + by) % peers) for i in range(peers)])


def passed_along(value, axis, steps):
    count = lax.axis_size(axis)
    first, last = (max(0, -steps), min(count, count - steps))
    return lax.ppermute(value, axis, [(source, source + steps) for source in range(first, last)])


def widen(value):
    return lax.all_gather(value, "tp", axis=1, tiled=True)


def norm_parts(x_full):
    xf = x_full.astype(jnp.float32)
    rms = jnp.sqrt(jnp.mean(xf * xf, axis=1, keepdims=True) + NORM_EPS)
    normed = xf / rms
    normed_b = normed.astype(jnp.bfloat16)
    return (xf, rms, normed, normed_b)


def forward_parts(x_full, wg, wu):
    xf, rms, normed, normed_b = norm_parts(x_full)
    gate = jnp.dot(normed_b, wg, preferred_element_type=jnp.float32) * (1.0 / math.sqrt(D))
    upper = jnp.dot(normed_b, wu, preferred_element_type=jnp.float32) * (1.0 / math.sqrt(D))
    return (xf, rms, normed, normed_b, gate, upper)


def adam_step(weight, first, second, grad):
    m_new = BETA_ONE * first.astype(jnp.float32) + (1.0 - BETA_ONE) * grad
    v_new = BETA_TWO * second.astype(jnp.float32) + (1.0 - BETA_TWO) * grad * grad
    return (weight.astype(jnp.float32) - LEARN * m_new / (jnp.sqrt(v_new) + ADAM_EPS)).astype(
        jnp.bfloat16
    )


def partner_mean(stacked, distance):
    other = jax.tree.map(
        lambda part, own: part.astype(own.dtype),
        from_behind(as_sent(stacked), "rep", distance),
        stacked,
    )
    return ((stacked.astype(jnp.float32) + other.astype(jnp.float32)) * 0.5).astype(jnp.bfloat16)


def contract(left, right, left_dim, right_dim):
    return lax.dot_general(
        left, right, (((left_dim,), (right_dim,)), ((), ())), preferred_element_type=jnp.float32
    )


def on_device(
    acts, cotangent, w_gate, w_up, w_down, m_gate, m_up, m_down, v_gate, v_up, v_down, steps
):
    section = lax.axis_index("section")
    sections = lax.axis_size("section")
    part = lax.axis_index("tp")
    local_width = acts.shape[2]
    wg = w_gate[0, 0]
    wu = w_up[0, 0]
    wd = w_down[0, 0]
    local_hidden = wg.shape[1]
    inv_ff = 1.0 / math.sqrt(FF)
    ticks = MB + sections - 1
    inputs = acts[0].reshape(MB, TOK, local_width)
    cots = cotangent[0].reshape(MB, TOK, local_width)
    saved = jnp.zeros((MB, TOK, D), jnp.bfloat16)
    gate_saved = jnp.zeros((MB, TOK, local_hidden), jnp.float32)
    upper_saved = jnp.zeros((MB, TOK, local_hidden), jnp.float32)
    out_buf = jnp.zeros((MB, TOK, local_width), jnp.bfloat16)
    incoming = jnp.zeros((TOK, local_width), jnp.bfloat16)
    for tick in range(ticks):
        micro = tick - section
        valid = (micro >= 0) & (micro < MB)
        place = jnp.clip(micro, 0, MB - 1)
        first = lax.dynamic_index_in_dim(inputs, place, 0, keepdims=False)
        x_local = jnp.where(section == 0, first, incoming)
        x_full = widen(x_local)
        xf, rms, normed, normed_b, gate, upper = forward_parts(x_full, wg, wu)
        hidden = (jax.nn.silu(gate) * upper).astype(jnp.bfloat16)
        partial_out = jnp.dot(hidden, wd, preferred_element_type=jnp.float32) * inv_ff
        share = lax.psum_scatter(
            partial_out.astype(jnp.bfloat16), "tp", scatter_dimension=1, tiled=True
        ).astype(jnp.float32)
        y_local = (x_local.astype(jnp.float32) + share).astype(jnp.bfloat16)
        if tick < ticks - 1:
            incoming = passed_along(y_local, "section", 1)
        saved = jnp.where(valid, lax.dynamic_update_index_in_dim(saved, x_full, place, 0), saved)
        gate_saved = jnp.where(
            valid, lax.dynamic_update_index_in_dim(gate_saved, gate, place, 0), gate_saved
        )
        upper_saved = jnp.where(
            valid, lax.dynamic_update_index_in_dim(upper_saved, upper, place, 0), upper_saved
        )
        out_buf = jnp.where(
            valid, lax.dynamic_update_index_in_dim(out_buf, y_local, place, 0), out_buf
        )
    acc_gate = jnp.zeros(wg.shape, jnp.float32)
    acc_up = jnp.zeros(wu.shape, jnp.float32)
    acc_down = jnp.zeros(wd.shape, jnp.float32)
    grad_buf = jnp.zeros((MB, TOK, local_width), jnp.bfloat16)
    incoming_back = jnp.zeros((TOK, local_width), jnp.bfloat16)
    for tick in range(ticks):
        micro = tick - (sections - 1 - section)
        valid = (micro >= 0) & (micro < MB)
        place = jnp.clip(micro, 0, MB - 1)
        last_cot = lax.dynamic_index_in_dim(cots, place, 0, keepdims=False)
        dy_local = jnp.where(section == sections - 1, last_cot, incoming_back)
        dy_full = widen(dy_local)
        x_full = lax.dynamic_index_in_dim(saved, place, 0, keepdims=False)
        xf, rms, normed, normed_b = norm_parts(x_full)
        gate = lax.dynamic_index_in_dim(gate_saved, place, 0, keepdims=False)
        upper = lax.dynamic_index_in_dim(upper_saved, place, 0, keepdims=False)
        sig = jax.nn.sigmoid(gate)
        active = gate * sig
        hidden = (active * upper).astype(jnp.bfloat16)
        dh = contract(dy_full, wd, 1, 1) * inv_ff
        dgate = (dh * upper * sig * (1.0 + gate * (1.0 - sig))).astype(jnp.bfloat16)
        dup = (dh * active).astype(jnp.bfloat16)
        acc_down = acc_down + jnp.where(valid, contract(hidden, dy_full, 0, 0) * inv_ff, 0.0)
        acc_gate = acc_gate + jnp.where(
            valid, contract(normed_b, dgate, 0, 0) * (1.0 / math.sqrt(D)), 0.0
        )
        acc_up = acc_up + jnp.where(
            valid, contract(normed_b, dup, 0, 0) * (1.0 / math.sqrt(D)), 0.0
        )
        partial_in = (contract(dgate, wg, 1, 1) + contract(dup, wu, 1, 1)) * (1.0 / math.sqrt(D))
        dnorm_local = lax.psum_scatter(
            partial_in.astype(jnp.bfloat16), "tp", scatter_dimension=1, tiled=True
        ).astype(jnp.float32)
        normed_local = lax.dynamic_slice_in_dim(normed, part * local_width, local_width, 1)
        stat = lax.psum(jnp.sum(dnorm_local * normed_local, axis=1), "tp") / D
        dx_local = (
            dy_local.astype(jnp.float32) + (dnorm_local - normed_local * stat[:, None]) / rms
        ).astype(jnp.bfloat16)
        grad_buf = jnp.where(
            valid, lax.dynamic_update_index_in_dim(grad_buf, dx_local, place, 0), grad_buf
        )
        if tick < ticks - 1:
            incoming_back = passed_along(dx_local, "section", -1)
    new_gate_local = adam_step(wg, m_gate[0, 0], v_gate[0, 0], acc_gate)
    new_up_local = adam_step(wu, m_up[0, 0], v_up[0, 0], acc_up)
    new_down_local = adam_step(wd, m_down[0, 0], v_down[0, 0], acc_down)
    flat_size = wg.shape[0] * wg.shape[1]
    stacked = jnp.stack(
        [
            new_gate_local.reshape(flat_size),
            new_up_local.reshape(flat_size),
            new_down_local.reshape(flat_size),
        ]
    )
    levels = lax.axis_size("rep").bit_length() - 1
    branches = [functools.partial(partner_mean, distance=2**level) for level in range(levels)]
    which = steps[0] % levels
    averaged = lax.switch(which, branches, stacked)
    new_gate = averaged[0].reshape(wg.shape)[None, None]
    new_up = averaged[1].reshape(wu.shape)[None, None]
    new_down = averaged[2].reshape(wd.shape)[None, None]
    section_out = out_buf.reshape(1, 1, MB * TOK, local_width)
    section_in_grad = grad_buf.reshape(1, 1, MB * TOK, local_width)
    return (section_out, section_in_grad, new_gate, new_up, new_down)


def solution(mesh):
    return jax.shard_map(
        on_device,
        mesh=mesh,
        in_specs=(
            P("rep", None, "tp"),
            P("rep", None, "tp"),
            P("section", "rep", None, "tp"),
            P("section", "rep", None, "tp"),
            P("section", "rep", "tp", None),
            P("section", "rep", None, "tp"),
            P("section", "rep", None, "tp"),
            P("section", "rep", "tp", None),
            P("section", "rep", None, "tp"),
            P("section", "rep", None, "tp"),
            P("section", "rep", "tp", None),
            P("section"),
        ),
        out_specs=(
            P("section", "rep", None, "tp"),
            P("section", "rep", None, "tp"),
            P("section", "rep", None, "tp"),
            P("section", "rep", None, "tp"),
            P("section", "rep", "tp", None),
        ),
        check_vma=False,
    )
```

profile of v0, /device:TPU:66, one launch (start us, length us, event | category | flops | bytes accessed | tf_op | source)
XLA Modules:
  0.0 1532.5 jit_solution(6093599195167706535)
XLA Ops:
  9.0 44.1 %all-gather = bf16[1,128,896]{1,2,0:T(8,128)(2,1)S(1)} all-gather(bf16[1,128,112]{1,2,0:T(8,128)(2,1)S(1)} %copy_select_fusion.1), channel_id=2, replica_groups=mesh['section'=4,'rep'=8,'tp'=8] {'tp'}, dimensions={2}, use_global_device_ids=true | all-gather | bytes 258048 | tf_op jit(solution)/shard_map/all_gather | solution.py:35
  59.2 76.5 %reduce-scatter.11.cloned.1.call-done = bf16[128,112]{0,1:T(8,128)(2,1)} async-done(((bf16[128,896]{0,1:T(8,128)(2,1)}), bf16[128,112]{0,1:T(8,128)(2,1)}) %reduce-scatter.11.cloned.1.call-update) | async-done | bytes 28688 | tf_op jit(solution)/shard_map/reduce_scatter | solution.py:106
  142.3 40.6 %all_gather.31 = bf16[128,896]{0,1:T(8,128)(2,1)S(1)} all-gather(bf16[128,112]{0,1:T(8,128)(2,1)S(1)} %bitcast_select_fusion.19), channel_id=1, replica_groups=mesh['section'=4,'rep'=8,'tp'=8] {'tp'}, dimensions={1}, use_global_device_ids=true | all-gather | bytes 258048 | tf_op jit(solution)/shard_map/all_gather | solution.py:35
  187.2 76.0 %reduce-scatter.13.cloned.1.call-done = bf16[128,112]{0,1:T(8,128)(2,1)} async-done(((bf16[128,896]{0,1:T(8,128)(2,1)}), bf16[128,112]{0,1:T(8,128)(2,1)}) %reduce-scatter.13.cloned.1.call-update) | async-done | bytes 28688 | tf_op jit(solution)/shard_map/reduce_scatter | solution.py:106
  269.8 40.6 %all_gather.32 = bf16[128,896]{0,1:T(8,128)(2,1)S(1)} all-gather(bf16[128,112]{0,1:T(8,128)(2,1)S(1)} %bitcast_select_fusion.18), channel_id=1, replica_groups=mesh['section'=4,'rep'=8,'tp'=8] {'tp'}, dimensions={1}, use_global_device_ids=true | all-gather | bytes 258048 | tf_op jit(solution)/shard_map/all_gather | solution.py:35
  315.4 75.3 %reduce-scatter.15.cloned.1.call-done = bf16[128,112]{0,1:T(8,128)(2,1)} async-done(((bf16[128,896]{0,1:T(8,128)(2,1)}), bf16[128,112]{0,1:T(8,128)(2,1)}) %reduce-scatter.15.cloned.1.call-update) | async-done | bytes 28688 | tf_op jit(solution)/shard_map/reduce_scatter | solution.py:106
  394.1 43.8 %all-gather.1 = bf16[1,128,896]{1,2,0:T(8,128)(2,1)} all-gather(bf16[1,128,112]{1,2,0:T(8,128)(2,1)} %copy_select_fusion), channel_id=3, replica_groups=mesh['section'=4,'rep'=8,'tp'=8] {'tp'}, dimensions={2}, use_global_device_ids=true | all-gather | bytes 258048 | tf_op jit(solution)/shard_map/all_gather | solution.py:35
  439.4 44.0 %all_gather.33 = bf16[128,896]{0,1:T(8,128)(2,1)S(1)} all-gather(bf16[128,112]{0,1:T(8,128)(2,1)S(1)} %bitcast_select_fusion.17), channel_id=1, replica_groups=mesh['section'=4,'rep'=8,'tp'=8] {'tp'}, dimensions={1}, use_global_device_ids=true | all-gather | bytes 258048 | tf_op jit(solution)/shard_map/all_gather | solution.py:35
  488.8 74.4 %reduce-scatter.17.cloned.1.call-done = bf16[128,112]{0,1:T(8,128)(2,1)} async-done(((bf16[128,896]{0,1:T(8,128)(2,1)}), bf16[128,112]{0,1:T(8,128)(2,1)}) %reduce-scatter.17.cloned.1.call-update) | async-done | bytes 28688 | tf_op jit(solution)/shard_map/reduce_scatter | solution.py:106
  570.6 41.1 %all_gather.34 = bf16[128,896]{0,1:T(8,128)(2,1)S(1)} all-gather(bf16[128,112]{0,1:T(8,128)(2,1)S(1)} %bitcast_select_fusion.16), channel_id=1, replica_groups=mesh['section'=4,'rep'=8,'tp'=8] {'tp'}, dimensions={1}, use_global_device_ids=true | all-gather | bytes 258048 | tf_op jit(solution)/shard_map/all_gather | solution.py:35
  630.5 69.0 %reduce-scatter.21.cloned.1.call-done = bf16[128,112]{0,1:T(8,128)(2,1)} async-done(((bf16[128,896]{0,1:T(8,128)(2,1)}), bf16[128,112]{0,1:T(8,128)(2,1)}) %reduce-scatter.21.cloned.1.call-update) | async-done | bytes 28688 | tf_op jit(solution)/shard_map/reduce_scatter | solution.py:152
  700.4 24.6 %psum.35 = f32[128]{0:T(128)S(1)} all-reduce(f32[128]{0:T(128)S(1)} %fusion.173), channel_id=1, replica_groups=mesh['section'=4,'rep'=8,'tp'=8] {'tp'}, use_global_device_ids=true, to_apply=%region_13.14 | all-reduce | flops 128 | bytes 1024 | tf_op jit(solution)/shard_map/psum | solution.py:156
  729.2 47.1 %reduce-scatter.19.cloned.1.call-done = bf16[128,112]{0,1:T(8,128)(2,1)} async-done(((bf16[128,896]{0,1:T(8,128)(2,1)}), bf16[128,112]{0,1:T(8,128)(2,1)}) %reduce-scatter.19.cloned.1.call-update) | async-done | bytes 28688 | tf_op jit(solution)/shard_map/reduce_scatter | solution.py:106
  779.1 40.6 %all_gather.36 = bf16[128,896]{0,1:T(8,128)(2,1)S(1)} all-gather(bf16[128,112]{0,1:T(8,128)(2,1)S(1)} %bitcast_select_fusion.15), channel_id=1, replica_groups=mesh['section'=4,'rep'=8,'tp'=8] {'tp'}, dimensions={1}, use_global_device_ids=true | all-gather | bytes 258048 | tf_op jit(solution)/shard_map/all_gather | solution.py:35
  829.7 70.5 %reduce-scatter.23.cloned.1.call-done = bf16[128,112]{0,1:T(8,128)(2,1)} async-done(((bf16[128,896]{0,1:T(8,128)(2,1)}), bf16[128,112]{0,1:T(8,128)(2,1)}) %reduce-scatter.23.cloned.1.call-update) | async-done | bytes 28688 | tf_op jit(solution)/shard_map/reduce_scatter | solution.py:152
  933.3 39.7 %all_gather.37 = bf16[128,896]{0,1:T(8,128)(2,1)S(1)} all-gather(bf16[128,112]{0,1:T(8,128)(2,1)S(1)} %bitcast_select_fusion.14), channel_id=1, replica_groups=mesh['section'=4,'rep'=8,'tp'=8] {'tp'}, dimensions={1}, use_global_device_ids=true | all-gather | bytes 258048 | tf_op jit(solution)/shard_map/all_gather | solution.py:35
  982.6 75.5 %reduce-scatter.25.cloned.1.call-done = bf16[128,112]{0,1:T(8,128)(2,1)} async-done(((bf16[128,896]{0,1:T(8,128)(2,1)}), bf16[128,112]{0,1:T(8,128)(2,1)}) %reduce-scatter.25.cloned.1.call-update) | async-done | bytes 28688 | tf_op jit(solution)/shard_map/reduce_scatter | solution.py:152
  1091.2 40.0 %all_gather.38 = bf16[128,896]{0,1:T(8,128)(2,1)S(1)} all-gather(bf16[128,112]{0,1:T(8,128)(2,1)S(1)} %bitcast_select_fusion.13), channel_id=1, replica_groups=mesh['section'=4,'rep'=8,'tp'=8] {'tp'}, dimensions={1}, use_global_device_ids=true | all-gather | bytes 258048 | tf_op jit(solution)/shard_map/all_gather | solution.py:35
  1140.9 75.4 %reduce-scatter.27.cloned.1.call-done = bf16[128,112]{0,1:T(8,128)(2,1)} async-done(((bf16[128,896]{0,1:T(8,128)(2,1)}), bf16[128,112]{0,1:T(8,128)(2,1)}) %reduce-scatter.27.cloned.1.call-update) | async-done | bytes 28688 | tf_op jit(solution)/shard_map/reduce_scatter | solution.py:152
  1248.7 39.9 %all_gather.39 = bf16[128,896]{0,1:T(8,128)(2,1)S(1)} all-gather(bf16[128,112]{0,1:T(8,128)(2,1)S(1)} %bitcast_select_fusion.12), channel_id=1, replica_groups=mesh['section'=4,'rep'=8,'tp'=8] {'tp'}, dimensions={1}, use_global_device_ids=true | all-gather | bytes 258048 | tf_op jit(solution)/shard_map/all_gather | solution.py:35
  1353.2 138.0 %conditional.2 = (bf16[3,544768]{1,0:T(4,128)(2,1)}, bf16[1,544768]{1,0:T(2,128)(2,1)}, bf16[1,544768]{1,0:T(2,128)(2,1)}, bf16[1,544768]{1,0:T(2,128)(2,1)}, bf...) conditional(s32[]{:T(128)} %clamp.3, ...), branch_computations={%region_30.31_spmd, %region_31.32_spmd, %region_32.33_spmd} | conditional | flops 8171520 | bytes 56655996
  1365.0 81.6 %collective-permute-done.2 = bf16[3,544768]{1,0:T(4,128)(2,1)S(1)} collective-permute-done((bf16[3,544768]{1,0:T(4,128)(2,1)S(1)}, bf16[3,544768]{1,0:T(4,128)(2,1)S(1)}, u32[]{:S(2)}, u32[]{:S(2)}) %collective-permute-start.2) | collective-permute-done | bytes 3268640 | tf_op jit(solution)/shard_map/cond/branch_2_fun/ppermute | solution.py:25
  1449.5 32.6 %fusion.237 = (bf16[544768]{0:T(1024)(128)(2,1)S(1)}, bf16[1,544768]{1,0:T(2,128)(2,1)}, bf16[544768]{0:T(1024)(128)(2,1)}, bf16[1,544768]{1,0:T(2,128)(2,1)}, b...) fusion(bf16[3,544768]{1,0:T(4,128)(2,1)S(1)} %add_multiply_fusion.2), kind=kLoop, calls=%fused_computation.386 | loop fusion | bytes 9805824 | tf_op jit(solution)/shard_map/slice | solution.py:182
  1492.3 31.5 %psum.39 = f32[128]{0:T(128)S(1)} all-reduce(f32[128]{0:T(128)S(1)} %fusion.189), channel_id=1, replica_groups=mesh['section'=4,'rep'=8,'tp'=8] {'tp'}, use_global_device_ids=true, to_apply=%region_29.30 | all-reduce | flops 128 | bytes 1024 | tf_op jit(solution)/shard_map/psum | solution.py:156
  (281 shorter events, 290.8 us)
Async XLA Ops:
  7.2 128.5 %reduce-scatter.11.cloned.1.call-start = ((), (), s32[]{:S(2)}) async-start(), calls=%async_computation.10 | async-start | bytes 258048 | tf_op jit(solution)/shard_map/reduce_scatter | solution.py:106
  59.2 124.3 %copy-start.3 = (bf16[1,1,896,608]{2,3,1,0:T(8,128)(2,1)S(1)}, bf16[1,1,896,608]{2,3,1,0:T(8,128)(2,1)}, u32[]{:S(2)}) copy-start(bf16[1,1,896,608]{2,3,1,0:T(8,128)(2,1)} %param.18) | copy-start | bytes 3268612
  59.2 204.0 %reduce-scatter.13.cloned.1.call-start = ((), (), s32[]{:S(2)}) async-start(), calls=%async_computation.11 | async-start | bytes 258048 | tf_op jit(solution)/shard_map/reduce_scatter | solution.py:106
  136.5 5.8 collective-permute-start.3
  187.1 203.6 %reduce-scatter.15.cloned.1.call-start = ((), (), s32[]{:S(2)}) async-start(), calls=%async_computation.12 | async-start | bytes 258048 | tf_op jit(solution)/shard_map/reduce_scatter | solution.py:106
  264.0 5.8 collective-permute-start.4
  314.6 248.6 %reduce-scatter.17.cloned.1.call-start = ((), (), s32[]{:S(2)}) async-start(), calls=%async_computation.13 | async-start | bytes 258048 | tf_op jit(solution)/shard_map/reduce_scatter | solution.py:106
  391.4 47.2 %collective-permute-start.5 = (bf16[128,112]{0,1:T(8,128)(2,1)S(1)}, bf16[128,112]{0,1:T(8,128)(2,1)S(1)}, u32[]{:S(2)}, u32[]{:S(2)}) collective-permute-start(bf16[128,112]{0,1:T(8,128)(2,1)S(1)} %get-tuple-element.80), channel_id=1, source_target_pairs={{0,64},{64,128},{128,192},{1,65},{65,129},{129,193},{2,66},{66,130... | collective-permute-start | bytes 86024 | tf_op jit(solution)/shard_map/ppermute | solution.py:31
  487.6 212.0 %reduce-scatter.21.cloned.1.call-start = ((), (), s32[]{:S(2)}) async-start(), calls=%async_computation.15 | async-start | bytes 258048 | tf_op jit(solution)/shard_map/reduce_scatter | solution.py:152
  564.0 5.8 collective-permute-start.6
  623.3 152.9 %reduce-scatter.19.cloned.1.call-start = ((), (), s32[]{:S(2)}) async-start(), calls=%async_computation.14 | async-start | bytes 258048 | tf_op jit(solution)/shard_map/reduce_scatter | solution.py:106
  629.0 147.2 %copy-start.19 = (bf16[2,128,112]{1,2,0:T(8,128)(2,1)S(1)}, bf16[2,128,112]{1,2,0:T(8,128)(2,1)}, u32[]{:S(2)}) copy-start(bf16[2,128,112]{1,2,0:T(8,128)(2,1)} %copy-done.18) | copy-start | bytes 172036
  629.0 147.2 %copy-start.29 = (bf16[128,112]{0,1:T(8,128)(2,1)S(1)}, bf16[128,112]{0,1:T(8,128)(2,1)}, u32[]{:S(2)}) copy-start(bf16[128,112]{0,1:T(8,128)(2,1)} %copy-done.28) | copy-start | bytes 86020
  629.0 148.7 %copy-start.39 = (bf16[1,128,112]{1,0,2:T(2,128)(2,1)S(1)}, bf16[1,128,112]{1,0,2:T(2,128)(2,1)}, u32[]{:S(2)}) copy-start(bf16[1,128,112]{1,0,2:T(2,128)(2,1)} %get-tuple-element.115) | copy-start | bytes 86020
  629.0 271.1 %reduce-scatter.23.cloned.1.call-start = ((), (), s32[]{:S(2)}) async-start(), calls=%async_computation.16 | async-start | bytes 258048 | tf_op jit(solution)/shard_map/reduce_scatter | solution.py:152
  725.9 51.8 %collective-permute-start.7 = (bf16[128,112]{0,1:T(8,128)(2,1)S(1)}, bf16[128,112]{0,1:T(8,128)(2,1)}, u32[]{:S(2)}, u32[]{:S(2)}) collective-permute-start(bf16[128,112]{0,1:T(8,128)(2,1)S(1)} %get-tuple-element.76), channel_id=1, source_target_pairs={{64,0},{128,64},{192,128},{65,1},{129,65},{193,129},{66,2},{130,66... | collective-permute-start | bytes 86024 | tf_op jit(solution)/shard_map/ppermute | solution.py:31
  824.0 234.1 %reduce-scatter.25.cloned.1.call-start = ((), (), s32[]{:S(2)}) async-start(), calls=%async_computation.17 | async-start | bytes 258048 | tf_op jit(solution)/shard_map/reduce_scatter | solution.py:152
  926.6 6.1 collective-permute-start.8
  977.0 239.3 %reduce-scatter.27.cloned.1.call-start = ((), (), s32[]{:S(2)}) async-start(), calls=%async_computation.18 | async-start | bytes 258048 | tf_op jit(solution)/shard_map/reduce_scatter | solution.py:152
  982.6 108.0 %copy-start.37 = (bf16[1,128,112]{1,0,2:T(2,128)(2,1)S(1)}, bf16[1,128,112]{1,0,2:T(2,128)(2,1)}, u32[]{:S(2)}) copy-start(bf16[1,128,112]{1,0,2:T(2,128)(2,1)} %get-tuple-element.113) | copy-start | bytes 86020
  1084.5 6.0 collective-permute-start.9
  1135.2 356.1 %reduce-scatter.29.cloned.1.call-start = ((), (), s32[]{:S(2)}) async-start(), calls=%async_computation.19 | async-start | bytes 258048 | tf_op jit(solution)/shard_map/reduce_scatter | solution.py:152
  1242.7 6.0 collective-permute-start.10
  1354.3 92.3 %collective-permute-start.2 = (bf16[3,544768]{1,0:T(4,128)(2,1)S(1)}, bf16[3,544768]{1,0:T(4,128)(2,1)S(1)}, u32[]{:S(2)}, u32[]{:S(2)}) collective-permute-start(bf16[3,544768]{1,0:T(4,128)(2,1)S(1)} %param.2), channel_id=1, source_target_pairs={{0,32},{8,40},{16,48},{24,56},{32,0},{40,8},{48,16},{56,24},{1,33}... | collective-permute-start | bytes 9805832 | tf_op jit(solution)/shard_map/cond/branch_2_fun/ppermute | solution.py:25
  (54 other events, 928.4 us)
Sparse Core Ops, SparseCore 0:
  59.3 76.3 reduce-scatter.10
  187.2 75.9 reduce-scatter.12
  314.7 75.9 reduce-scatter.14
  487.7 75.4 reduce-scatter.16
  623.5 76.0 reduce-scatter.20
  703.1 73.1 reduce-scatter.18
  824.1 76.0 reduce-scatter.22
  977.2 80.9 reduce-scatter.24
  1135.3 80.9 reduce-scatter.26
  1292.2 80.7 reduce-scatter.28
where the time goes:
time: 1540 us; the launch traced here: 1530 us
  waiting for transfers between devices  729 us (47%)
  blocking collectives  544 us (35%)
  local copies, waits for them, and re-layouts  88.1 us (6%)
  matrix products  87.2 us (6%)
  starting transfers between devices  34.7 us (2%)
  other arithmetic  32.1 us (2%)
  between operations  16 us (1%)
    all_gather x10, blocking collectives, widen(): return lax.all_gather(value, 'tp', axis=1, tiled=True)  414 us
    reduce_scatter x5, waiting for transfers between devices, on_device(): lax.psum_scatter(partial_out.astype(jnp.bfloat16), 'tp', scatter_dimensio...  349 us
    reduce_scatter x5, waiting for transfers between devices, on_device(): lax.psum_scatter(partial_in.astype(jnp.bfloat16), 'tp', scatter_dimension...  290 us
    psum x5, blocking collectives, on_device(): stat = lax.psum(jnp.sum(dnorm_local * normed_local, axis=1), 'tp') / D  130 us
    ppermute x1, waiting for transfers between devices, from_behind(): lax.ppermute(array, axis, [(i, (i + by) % peers) for i in range(peers)])  81.6 us
    dot_general x30, matrix products, contract(): lax.dot_general(left, right, (((left_dim,), (right_dim,)), ((), ())), pre...  64.8 us
    slice x1, local copies, waits for them, and re-layouts, on_device(): new_down = averaged[2].reshape(wd.shape)[None, None]  32.6 us
  transfers between devices with their start and end apart: 19, of which 13 were waited for; matrix products, arithmetic and copies ran while one was open for 9% of the time, Pallas kernels for 0%

commit v1 on v0

--- a/solution.py
+++ b/solution.py
@@ -14,6 +14,11 @@
 LEARN = 0.3
 BETA_ONE = 0.9
 BETA_TWO = 0.95
+
+
+def summed_here(block, axis):
+    terms = lax.all_gather(block, axis)
+    return jnp.sum(terms, axis=0)
 
 
 def as_sent(array):
@@ -153,7 +158,7 @@
             partial_in.astype(jnp.bfloat16), "tp", scatter_dimension=1, tiled=True
         ).astype(jnp.float32)
         normed_local = lax.dynamic_slice_in_dim(normed, part * local_width, local_width, 1)
-        stat = lax.psum(jnp.sum(dnorm_local * normed_local, axis=1), "tp") / D
+        stat = summed_here(jnp.sum(dnorm_local * normed_local, axis=1), "tp") / D
         dx_local = (
             dy_local.astype(jnp.float32) + (dnorm_local - normed_local * stat[:, None]) / rms
         ).astype(jnp.bfloat16)

time: 1540 us -> 1530 us (level)
    psum x5 -> x0, blocking collectives: 130 us -> none  [on_device(): stat = lax.psum(jnp.sum(dnorm_local * normed_local, axis=1), 'tp') / D]
    all_gather x0 -> x5, blocking collectives: none -> 125 us  [summed_here(): terms = lax.all_gather(block, axis)]
where the time goes in v1:
time: 1530 us
  waiting for transfers between devices  729 us (48%)
  blocking collectives  540 us (35%)
  matrix products  87.3 us (6%)
  local copies, waits for them, and re-layouts  85.3 us (6%)
  starting transfers between devices  34.7 us (2%)
  other arithmetic  32.2 us (2%)
  between operations  16 us (1%)
    all_gather x10, blocking collectives, widen(): return lax.all_gather(value, 'tp', axis=1, tiled=True)  415 us
    reduce_scatter x5, waiting for transfers between devices, on_device(): lax.psum_scatter(partial_out.astype(jnp.bfloat16), 'tp', scatter_dimensio...  350 us
    reduce_scatter x5, waiting for transfers between devices, on_device(): lax.psum_scatter(partial_in.astype(jnp.bfloat16), 'tp', scatter_dimension...  290 us
    all_gather x5, blocking collectives, summed_here(): terms = lax.all_gather(block, axis)  125 us
    ppermute x1, waiting for transfers between devices, from_behind(): lax.ppermute(array, axis, [(i, (i + by) % peers) for i in range(peers)])  81.4 us
    dot_general x30, matrix products, contract(): lax.dot_general(left, right, (((left_dim,), (right_dim,)), ((), ())), pre...  64.9 us
    slice x1, local copies, waits for them, and re-layouts, on_device(): new_down = averaged[2].reshape(wd.shape)[None, None]  31.7 us
  transfers between devices with their start and end apart: 19, of which 13 were waited for; matrix products, arithmetic and copies ran while one was open for 9% of the time, Pallas kernels for 0%

profile of v1, /device:TPU:66, one launch (start us, length us, event | category | flops | bytes accessed | tf_op | source)
XLA Modules:
  0.0 1526.2 jit_solution(10482373815532284132)
XLA Ops:
  9.0 44.1 %all-gather = bf16[1,128,896]{1,2,0:T(8,128)(2,1)S(1)} all-gather(bf16[1,128,112]{1,2,0:T(8,128)(2,1)S(1)} %copy_select_fusion.1), channel_id=2, replica_groups=mesh['section'=4,'rep'=8,'tp'=8] {'tp'}, dimensions={2}, use_global_device_ids=true | all-gather | bytes 258048 | tf_op jit(solution)/shard_map/all_gather | solution.py:40
  59.2 76.5 %reduce-scatter.11.cloned.1.call-done = bf16[128,112]{0,1:T(8,128)(2,1)} async-done(((bf16[128,896]{0,1:T(8,128)(2,1)}), bf16[128,112]{0,1:T(8,128)(2,1)}) %reduce-scatter.11.cloned.1.call-update) | async-done | bytes 28688 | tf_op jit(solution)/shard_map/reduce_scatter | solution.py:111
  142.3 40.6 %all_gather.61 = bf16[128,896]{0,1:T(8,128)(2,1)S(1)} all-gather(bf16[128,112]{0,1:T(8,128)(2,1)S(1)} %bitcast_select_fusion.19), channel_id=1, replica_groups=mesh['section'=4,'rep'=8,'tp'=8] {'tp'}, dimensions={1}, use_global_device_ids=true | all-gather | bytes 258048 | tf_op jit(solution)/shard_map/all_gather | solution.py:40
  187.2 76.0 %reduce-scatter.13.cloned.1.call-done = bf16[128,112]{0,1:T(8,128)(2,1)} async-done(((bf16[128,896]{0,1:T(8,128)(2,1)}), bf16[128,112]{0,1:T(8,128)(2,1)}) %reduce-scatter.13.cloned.1.call-update) | async-done | bytes 28688 | tf_op jit(solution)/shard_map/reduce_scatter | solution.py:111
  269.8 40.6 %all_gather.62 = bf16[128,896]{0,1:T(8,128)(2,1)S(1)} all-gather(bf16[128,112]{0,1:T(8,128)(2,1)S(1)} %bitcast_select_fusion.18), channel_id=1, replica_groups=mesh['section'=4,'rep'=8,'tp'=8] {'tp'}, dimensions={1}, use_global_device_ids=true | all-gather | bytes 258048 | tf_op jit(solution)/shard_map/all_gather | solution.py:40
  315.4 75.3 %reduce-scatter.15.cloned.1.call-done = bf16[128,112]{0,1:T(8,128)(2,1)} async-done(((bf16[128,896]{0,1:T(8,128)(2,1)}), bf16[128,112]{0,1:T(8,128)(2,1)}) %reduce-scatter.15.cloned.1.call-update) | async-done | bytes 28688 | tf_op jit(solution)/shard_map/reduce_scatter | solution.py:111
  394.1 43.7 %all-gather.1 = bf16[1,128,896]{1,2,0:T(8,128)(2,1)} all-gather(bf16[1,128,112]{1,2,0:T(8,128)(2,1)} %copy_select_fusion), channel_id=3, replica_groups=mesh['section'=4,'rep'=8,'tp'=8] {'tp'}, dimensions={2}, use_global_device_ids=true | all-gather | bytes 258048 | tf_op jit(solution)/shard_map/all_gather | solution.py:40
  439.3 44.0 %all_gather.63 = bf16[128,896]{0,1:T(8,128)(2,1)S(1)} all-gather(bf16[128,112]{0,1:T(8,128)(2,1)S(1)} %bitcast_select_fusion.17), channel_id=1, replica_groups=mesh['section'=4,'rep'=8,'tp'=8] {'tp'}, dimensions={1}, use_global_device_ids=true | all-gather | bytes 258048 | tf_op jit(solution)/shard_map/all_gather | solution.py:40
  488.7 74.5 %reduce-scatter.17.cloned.1.call-done = bf16[128,112]{0,1:T(8,128)(2,1)} async-done(((bf16[128,896]{0,1:T(8,128)(2,1)}), bf16[128,112]{0,1:T(8,128)(2,1)}) %reduce-scatter.17.cloned.1.call-update) | async-done | bytes 28688 | tf_op jit(solution)/shard_map/reduce_scatter | solution.py:111
  570.6 41.1 %all_gather.64 = bf16[128,896]{0,1:T(8,128)(2,1)S(1)} all-gather(bf16[128,112]{0,1:T(8,128)(2,1)S(1)} %bitcast_select_fusion.16), channel_id=1, replica_groups=mesh['section'=4,'rep'=8,'tp'=8] {'tp'}, dimensions={1}, use_global_device_ids=true | all-gather | bytes 258048 | tf_op jit(solution)/shard_map/all_gather | solution.py:40
  630.6 69.0 %reduce-scatter.21.cloned.1.call-done = bf16[128,112]{0,1:T(8,128)(2,1)} async-done(((bf16[128,896]{0,1:T(8,128)(2,1)}), bf16[128,112]{0,1:T(8,128)(2,1)}) %reduce-scatter.21.cloned.1.call-update) | async-done | bytes 28688 | tf_op jit(solution)/shard_map/reduce_scatter | solution.py:157
  728.3 47.9 %reduce-scatter.19.cloned.1.call-done = bf16[128,112]{0,1:T(8,128)(2,1)} async-done(((bf16[128,896]{0,1:T(8,128)(2,1)}), bf16[128,112]{0,1:T(8,128)(2,1)}) %reduce-scatter.19.cloned.1.call-update) | async-done | bytes 28688 | tf_op jit(solution)/shard_map/reduce_scatter | solution.py:111
  779.1 40.7 %all_gather.68 = bf16[128,896]{0,1:T(8,128)(2,1)S(1)} all-gather(bf16[128,112]{0,1:T(8,128)(2,1)S(1)} %bitcast_select_fusion.15), channel_id=1, replica_groups=mesh['section'=4,'rep'=8,'tp'=8] {'tp'}, dimensions={1}, use_global_device_ids=true | all-gather | bytes 258048 | tf_op jit(solution)/shard_map/all_gather | solution.py:40
  829.7 70.4 %reduce-scatter.23.cloned.1.call-done = bf16[128,112]{0,1:T(8,128)(2,1)} async-done(((bf16[128,896]{0,1:T(8,128)(2,1)}), bf16[128,112]{0,1:T(8,128)(2,1)}) %reduce-scatter.23.cloned.1.call-update) | async-done | bytes 28688 | tf_op jit(solution)/shard_map/reduce_scatter | solution.py:157
  901.0 23.7 %all-gather.8 = f32[8,1,128]{2,1,0:T(1,128)S(1)} all-gather(f32[1,1,128]{2,1,0:T(1,128)S(1)} %bitcast.540), channel_id=5, replica_groups=mesh['section'=4,'rep'=8,'tp'=8] {'tp'}, dimensions={0}, use_global_device_ids=true | all-gather | bytes 4608 | tf_op jit(solution)/shard_map/all_gather | solution.py:20
  932.4 40.0 %all_gather.71 = bf16[128,896]{0,1:T(8,128)(2,1)S(1)} all-gather(bf16[128,112]{0,1:T(8,128)(2,1)S(1)} %bitcast_select_fusion.14), channel_id=1, replica_groups=mesh['section'=4,'rep'=8,'tp'=8] {'tp'}, dimensions={1}, use_global_device_ids=true | all-gather | bytes 258048 | tf_op jit(solution)/shard_map/all_gather | solution.py:40
  982.0 75.3 %reduce-scatter.25.cloned.1.call-done = bf16[128,112]{0,1:T(8,128)(2,1)} async-done(((bf16[128,896]{0,1:T(8,128)(2,1)}), bf16[128,112]{0,1:T(8,128)(2,1)}) %reduce-scatter.25.cloned.1.call-update) | async-done | bytes 28688 | tf_op jit(solution)/shard_map/reduce_scatter | solution.py:157
  1089.6 39.9 %all_gather.74 = bf16[128,896]{0,1:T(8,128)(2,1)S(1)} all-gather(bf16[128,112]{0,1:T(8,128)(2,1)S(1)} %bitcast_select_fusion.13), channel_id=1, replica_groups=mesh['section'=4,'rep'=8,'tp'=8] {'tp'}, dimensions={1}, use_global_device_ids=true | all-gather | bytes 258048 | tf_op jit(solution)/shard_map/all_gather | solution.py:40
  1139.2 75.4 %reduce-scatter.27.cloned.1.call-done = bf16[128,112]{0,1:T(8,128)(2,1)} async-done(((bf16[128,896]{0,1:T(8,128)(2,1)}), bf16[128,112]{0,1:T(8,128)(2,1)}) %reduce-scatter.27.cloned.1.call-update) | async-done | bytes 28688 | tf_op jit(solution)/shard_map/reduce_scatter | solution.py:157
  1246.2 40.0 %all_gather.77 = bf16[128,896]{0,1:T(8,128)(2,1)S(1)} all-gather(bf16[128,112]{0,1:T(8,128)(2,1)S(1)} %bitcast_select_fusion.12), channel_id=1, replica_groups=mesh['section'=4,'rep'=8,'tp'=8] {'tp'}, dimensions={1}, use_global_device_ids=true | all-gather | bytes 258048 | tf_op jit(solution)/shard_map/all_gather | solution.py:40
  1350.0 135.9 %conditional.2 = (bf16[3,544768]{1,0:T(4,128)(2,1)}, bf16[1,544768]{1,0:T(2,128)(2,1)}, bf16[1,544768]{1,0:T(2,128)(2,1)}, bf16[1,544768]{1,0:T(2,128)(2,1)}, bf...) conditional(s32[]{:T(128)} %clamp.3, ...), branch_computations={%region_30.31_spmd, %region_31.32_spmd, %region_32.33_spmd} | conditional | flops 8171520 | bytes 56655996
  1361.8 81.4 %collective-permute-done.2 = bf16[3,544768]{1,0:T(4,128)(2,1)S(1)} collective-permute-done((bf16[3,544768]{1,0:T(4,128)(2,1)S(1)}, bf16[3,544768]{1,0:T(4,128)(2,1)S(1)}, u32[]{:S(2)}, u32[]{:S(2)}) %collective-permute-start.2) | collective-permute-done | bytes 3268640 | tf_op jit(solution)/shard_map/cond/branch_2_fun/ppermute | solution.py:30
  1446.1 31.7 %fusion.237 = (bf16[544768]{0:T(1024)(128)(2,1)S(1)}, bf16[1,544768]{1,0:T(2,128)(2,1)}, bf16[544768]{0:T(1024)(128)(2,1)S(1)}, bf16[1,544768]{1,0:T(2,128)(2,1)...) fusion(bf16[3,544768]{1,0:T(4,128)(2,1)S(1)} %add_multiply_fusion.2), kind=kLoop, calls=%fused_computation.386 | loop fusion | bytes 9805824 | tf_op jit(solution)/shard_map/slice | solution.py:187
  1487.0 30.5 %all-gather.11 = f32[8,1,128]{2,1,0:T(1,128)S(1)} all-gather(f32[1,1,128]{2,1,0:T(1,128)S(1)} %bitcast.543), channel_id=8, replica_groups=mesh['section'=4,'rep'=8,'tp'=8] {'tp'}, dimensions={0}, use_global_device_ids=true | all-gather | bytes 4608 | tf_op jit(solution)/shard_map/all_gather | solution.py:20
  (288 shorter events, 286.5 us)
Async XLA Ops:
  7.2 128.5 %reduce-scatter.11.cloned.1.call-start = ((), (), s32[]{:S(2)}) async-start(), calls=%async_computation.10 | async-start | bytes 258048 | tf_op jit(solution)/shard_map/reduce_scatter | solution.py:111
  59.2 124.3 %copy-start.3 = (bf16[1,1,896,608]{2,3,1,0:T(8,128)(2,1)S(1)}, bf16[1,1,896,608]{2,3,1,0:T(8,128)(2,1)}, u32[]{:S(2)}) copy-start(bf16[1,1,896,608]{2,3,1,0:T(8,128)(2,1)} %param.18) | copy-start | bytes 3268612
  59.2 204.0 %reduce-scatter.13.cloned.1.call-start = ((), (), s32[]{:S(2)}) async-start(), calls=%async_computation.11 | async-start | bytes 258048 | tf_op jit(solution)/shard_map/reduce_scatter | solution.py:111
  136.5 5.8 collective-permute-start.3
  187.1 203.6 %reduce-scatter.15.cloned.1.call-start = ((), (), s32[]{:S(2)}) async-start(), calls=%async_computation.12 | async-start | bytes 258048 | tf_op jit(solution)/shard_map/reduce_scatter | solution.py:111
  264.0 5.8 collective-permute-start.4
  314.5 248.7 %reduce-scatter.17.cloned.1.call-start = ((), (), s32[]{:S(2)}) async-start(), calls=%async_computation.13 | async-start | bytes 258048 | tf_op jit(solution)/shard_map/reduce_scatter | solution.py:111
  391.5 47.0 %collective-permute-start.5 = (bf16[128,112]{0,1:T(8,128)(2,1)S(1)}, bf16[128,112]{0,1:T(8,128)(2,1)S(1)}, u32[]{:S(2)}, u32[]{:S(2)}) collective-permute-start(bf16[128,112]{0,1:T(8,128)(2,1)S(1)} %get-tuple-element.85), channel_id=1, source_target_pairs={{0,64},{64,128},{128,192},{1,65},{65,129},{129,193},{2,66},{66,130... | collective-permute-start | bytes 86024 | tf_op jit(solution)/shard_map/ppermute | solution.py:36
  487.5 212.0 %reduce-scatter.21.cloned.1.call-start = ((), (), s32[]{:S(2)}) async-start(), calls=%async_computation.15 | async-start | bytes 258048 | tf_op jit(solution)/shard_map/reduce_scatter | solution.py:157
  564.0 5.8 collective-permute-start.6
  623.4 152.8 %reduce-scatter.19.cloned.1.call-start = ((), (), s32[]{:S(2)}) async-start(), calls=%async_computation.14 | async-start | bytes 258048 | tf_op jit(solution)/shard_map/reduce_scatter | solution.py:111
  629.1 147.2 %copy-start.19 = (bf16[2,128,112]{1,2,0:T(8,128)(2,1)S(1)}, bf16[2,128,112]{1,2,0:T(8,128)(2,1)}, u32[]{:S(2)}) copy-start(bf16[2,128,112]{1,2,0:T(8,128)(2,1)} %copy-done.18) | copy-start | bytes 172036
  629.1 147.2 %copy-start.29 = (bf16[128,112]{0,1:T(8,128)(2,1)S(1)}, bf16[128,112]{0,1:T(8,128)(2,1)}, u32[]{:S(2)}) copy-start(bf16[128,112]{0,1:T(8,128)(2,1)} %copy-done.28) | copy-start | bytes 86020
  629.1 148.6 %copy-start.39 = (bf16[1,128,112]{1,0,2:T(2,128)(2,1)S(1)}, bf16[1,128,112]{1,0,2:T(2,128)(2,1)}, u32[]{:S(2)}) copy-start(bf16[1,128,112]{1,0,2:T(2,128)(2,1)} %get-tuple-element.120) | copy-start | bytes 86020
  629.1 271.0 %reduce-scatter.23.cloned.1.call-start = ((), (), s32[]{:S(2)}) async-start(), calls=%async_computation.16 | async-start | bytes 258048 | tf_op jit(solution)/shard_map/reduce_scatter | solution.py:157
  725.1 52.7 %collective-permute-start.7 = (bf16[128,112]{0,1:T(8,128)(2,1)S(1)}, bf16[128,112]{0,1:T(8,128)(2,1)}, u32[]{:S(2)}, u32[]{:S(2)}) collective-permute-start(bf16[128,112]{0,1:T(8,128)(2,1)S(1)} %get-tuple-element.81), channel_id=1, source_target_pairs={{64,0},{128,64},{192,128},{65,1},{129,65},{193,129},{66,2},{130,66... | collective-permute-start | bytes 86024 | tf_op jit(solution)/shard_map/ppermute | solution.py:36
  824.1 233.2 %reduce-scatter.25.cloned.1.call-start = ((), (), s32[]{:S(2)}) async-start(), calls=%async_computation.17 | async-start | bytes 258048 | tf_op jit(solution)/shard_map/reduce_scatter | solution.py:157
  925.7 6.1 collective-permute-start.8
  976.4 238.1 %reduce-scatter.27.cloned.1.call-start = ((), (), s32[]{:S(2)}) async-start(), calls=%async_computation.18 | async-start | bytes 258048 | tf_op jit(solution)/shard_map/reduce_scatter | solution.py:157
  982.0 107.0 %copy-start.37 = (bf16[1,128,112]{1,0,2:T(2,128)(2,1)S(1)}, bf16[1,128,112]{1,0,2:T(2,128)(2,1)}, u32[]{:S(2)}) copy-start(bf16[1,128,112]{1,0,2:T(2,128)(2,1)} %get-tuple-element.118) | copy-start | bytes 86020
  1082.9 6.2 collective-permute-start.9
  1133.6 352.5 %reduce-scatter.29.cloned.1.call-start = ((), (), s32[]{:S(2)}) async-start(), calls=%async_computation.19 | async-start | bytes 258048 | tf_op jit(solution)/shard_map/reduce_scatter | solution.py:157
  1240.2 6.0 collective-permute-start.10
  1351.1 92.0 %collective-permute-start.2 = (bf16[3,544768]{1,0:T(4,128)(2,1)S(1)}, bf16[3,544768]{1,0:T(4,128)(2,1)S(1)}, u32[]{:S(2)}, u32[]{:S(2)}) collective-permute-start(bf16[3,544768]{1,0:T(4,128)(2,1)S(1)} %param.2), channel_id=1, source_target_pairs={{0,32},{8,40},{16,48},{24,56},{32,0},{40,8},{48,16},{56,24},{1,33}... | collective-permute-start | bytes 9805832 | tf_op jit(solution)/shard_map/cond/branch_2_fun/ppermute | solution.py:30
  (55 other events, 925.9 us)
Sparse Core Ops, SparseCore 0:
  59.3 76.3 reduce-scatter.10
  187.2 75.9 reduce-scatter.12
  314.7 75.9 reduce-scatter.14
  487.7 75.4 reduce-scatter.16
  623.5 75.9 reduce-scatter.20
  703.1 73.0 reduce-scatter.18
  824.2 75.8 reduce-scatter.22
  976.5 80.6 reduce-scatter.24
  1133.7 80.8 reduce-scatter.26
  1290.5 80.6 reduce-scatter.28
